TPU v7x, 32 devices: a whole 2x2x4 slice. The times are simulated.
32 devices in a mesh: grp: 2 (over x), tok: 4 (over y, core), feat: 4 (over z).
Axes of the slice: x: 2, y: 2, z: 4, core: 2. Of those that a mesh axis runs over, the one named last changes fastest.
Arguments:
- activations: bfloat16 [4096, 3072], P(('grp', 'tok', 'feat')), parts along dimension 0, may hold values from -6 to 6
- block_lists: int32 [2048, 4], P(('grp', 'tok', 'feat')), parts along dimension 0, may hold values from 0 to 15, as said below
- top_positions: int32 [4096, 64], P(('grp', 'tok', 'feat')), parts along dimension 0, may hold values from 0 to 2047, as said below
- enc_weight: bfloat16 [3072, 8192], P(None, ('tok', 'feat')), may hold values from -0.109375 to 0.109375
- enc_bias: float32 [8192], P(('tok', 'feat')), may hold values from -3 to 3
- dec_weight: bfloat16 [8192, 3072], P(('tok', 'feat')), may hold values from -2.5 to 2.5
- dec_bias: float32 [3072], replicated, may hold values from -6 to 6
Outputs:
- enc_grad: bfloat16 [3072, 16384], P(None, ('grp', 'tok', 'feat')), parts along dimension 1
- dec_grad: bfloat16 [16384, 3072], P(('grp', 'tok', 'feat')), parts along dimension 0
There are 2 independent parts, one for each index of `grp`. A program takes and returns all parts, laid end to end along the dimension named above; an argument that names none is the same for every part. Nothing has to cross between parts.
Inputs may be any that keep to these rules, and one draw needn't show every extreme that they name: `block_lists`: each row block names 4 different feature blocks. In the aligned blocks of 64 rows that one device holds, no feature block is named more than 24 times. In every draw one feature block is named exactly 24 times in every such block of rows. `top_positions`: the 64 entries of a token are distinct.
All inputs are finite; a program needn't handle non-finite values.
Results may differ from a plain program's by a relative error of at most 0.0058.
Values may be sent and summed in bfloat16 or wider, within the bound.
A program may use at most 128 MiB of HBM per device.

v0:
```python
import jax
import jax.numpy as jnp
from jax import lax
from jax.sharding import PartitionSpec as P


def dispatch_rows(send_x, send_rel):
    result = (
        lax.all_to_all(send_x, ("tok", "feat"), split_axis=0, concat_axis=0, tiled=True),
        lax.all_to_all(send_rel, ("tok", "feat"), split_axis=0, concat_axis=0, tiled=True),
    )
    return result


def return_partials(partial_value):
    result = lax.all_to_all(partial_value, ("tok", "feat"), split_axis=0, concat_axis=0, tiled=True)
    return result


def dispatch_errors(send_err):
    result = lax.all_to_all(send_err, ("tok", "feat"), split_axis=0, concat_axis=0, tiled=True)
    return result


def routed_plan(
    activations, block_lists, top_positions, enc_weight, enc_bias, dec_weight, dec_bias
):
    owner_count = lax.axis_size(("tok", "feat"))
    token_count, model_width = activations.shape
    block_rows, active_count = block_lists.shape
    group_rows = token_count // block_rows
    feat_block = enc_weight.shape[1]
    top_count = top_positions.shape[1]
    slot_count = max(2, 3 * token_count * active_count // (2 * group_rows * owner_count))
    per_owner = slot_count * group_rows
    buffer_rows = owner_count * per_owner
    pair_count = block_rows * active_count
    pair_ids = block_lists.reshape(pair_count)
    pair_order = jnp.arange(pair_count, dtype=jnp.int32)
    earlier = (pair_ids[:, None] == pair_ids[None, :]) & (pair_order[None, :] < pair_order[:, None])
    pair_rank = jnp.sum(earlier.astype(jnp.int32), axis=1)
    lane_index = jnp.arange(group_rows, dtype=jnp.int32)
    target = (
        (pair_ids * per_owner + pair_rank * group_rows)[:, None] + lane_index[None, :]
    ).reshape(-1)
    source = ((pair_order // active_count * group_rows)[:, None] + lane_index[None, :]).reshape(-1)
    column = jnp.repeat(pair_order % active_count, group_rows)
    slot_index = jnp.arange(buffer_rows, dtype=jnp.int32)
    hit_bool = slot_index[:, None] == target[None, :]
    hit_float = hit_bool.astype(jnp.float32)
    place_float = jnp.sum(
        hit_float.reshape(buffer_rows, block_rows, active_count, group_rows), axis=2
    ).reshape(buffer_rows, token_count)
    place = place_float.astype(jnp.bfloat16)
    filled = jnp.sum(place_float, axis=1)
    send_x = jnp.dot(place, activations, preferred_element_type=jnp.float32).astype(jnp.bfloat16)
    offsets = top_positions[source] - column[:, None] * feat_block
    offsets = jnp.where((offsets >= 0) & (offsets < feat_block), offsets, feat_block)
    rel_float = (
        jnp.dot(hit_float, offsets.astype(jnp.float32), precision=lax.Precision.HIGHEST)
        + (1.0 - filled)[:, None] * feat_block
    )
    send_rel = rel_float.astype(jnp.int32)
    recv_x, recv_rel = dispatch_rows(
        send_x.reshape(owner_count, per_owner, model_width),
        send_rel.reshape(owner_count, per_owner, top_count),
    )
    recv_x = recv_x.reshape(buffer_rows, model_width)
    recv_rel = recv_rel.reshape(buffer_rows, top_count)
    feature_iota = jnp.arange(feat_block, dtype=jnp.int32)
    mask_bool = jnp.zeros((buffer_rows, feat_block), jnp.bool_)
    for begin in range(0, top_count, 8):
        piece = recv_rel[:, begin : begin + 8]
        mask_bool = mask_bool | jnp.any(piece[:, :, None] == feature_iota[None, None, :], axis=1)
    feat_mask = mask_bool.astype(jnp.float32)
    pre_acts = jnp.dot(recv_x, enc_weight, preferred_element_type=jnp.float32) + enc_bias
    code_vals = (feat_mask * pre_acts).astype(jnp.bfloat16)
    partial_value = jnp.dot(code_vals, dec_weight, preferred_element_type=jnp.float32).astype(
        jnp.bfloat16
    )
    returned = return_partials(partial_value.reshape(owner_count, per_owner, model_width)).reshape(
        buffer_rows, model_width
    )
    summed = lax.dot_general(
        place, returned, (((0,), (0,)), ((), ())), preferred_element_type=jnp.float32
    )
    residual = (summed + dec_bias - activations.astype(jnp.float32)).astype(jnp.bfloat16)
    send_err = jnp.dot(place, residual, preferred_element_type=jnp.float32).astype(jnp.bfloat16)
    recv_err = dispatch_errors(send_err.reshape(owner_count, per_owner, model_width)).reshape(
        buffer_rows, model_width
    )
    grad_codes = lax.dot_general(
        recv_err, dec_weight, (((1,), (1,)), ((), ())), preferred_element_type=jnp.float32
    )
    grad_pre = (feat_mask * grad_codes).astype(jnp.bfloat16)
    enc_grad = lax.dot_general(
        recv_x, grad_pre, (((0,), (0,)), ((), ())), preferred_element_type=jnp.float32
    ).astype(jnp.bfloat16)
    raw_grad = lax.dot_general(
        code_vals, recv_err, (((0,), (0,)), ((), ())), preferred_element_type=jnp.float32
    )
    dec_float = dec_weight.astype(jnp.float32)
    along_coef = jnp.sum(raw_grad * dec_float, axis=1) / (
        jnp.sum(dec_float * dec_float, axis=1) + 1e-06
    )
    dec_grad = (raw_grad - along_coef[:, None] * dec_float).astype(jnp.bfloat16)
    return (enc_grad, dec_grad)


GROUP = ("tok", "feat")


def global_ids(block_lists, top_positions, feat_block):
    token_count = top_positions.shape[0]
    block_rows, active_count = block_lists.shape
    lists = jnp.repeat(block_lists, token_count // block_rows, axis=0)
    column = top_positions // feat_block
    chosen = jnp.zeros_like(top_positions)
    for k in range(active_count):
        chosen = jnp.where(column == k, lists[:, k : k + 1], chosen)
    return chosen * feat_block + top_positions % feat_block


def select_mask(rel, feat_block):
    words = feat_block // 8
    inside = (rel >= 0) & (rel < feat_block)
    word = jnp.where(inside, rel // 8, words)
    bit = jnp.left_shift(1, rel & 7)
    word_iota = jnp.arange(words, dtype=jnp.int32)
    packed = jnp.sum(
        jnp.where(word[:, :, None] == word_iota[None, None, :], bit[:, :, None], 0), axis=1
    )
    feature_iota = jnp.arange(feat_block, dtype=jnp.int32)
    spread = (word_iota[:, None] == (feature_iota // 8)[None, :]).astype(jnp.bfloat16)
    wide = jnp.dot(
        packed.astype(jnp.float32).astype(jnp.bfloat16), spread, preferred_element_type=jnp.float32
    ).astype(jnp.int32)
    return (jnp.right_shift(wide, (feature_iota & 7)[None, :]) & 1).astype(jnp.bfloat16)


def gathered_plan(
    activations, block_lists, top_positions, enc_weight, enc_bias, dec_weight, dec_bias
):
    feat_block = enc_weight.shape[1]
    ids = global_ids(block_lists, top_positions, feat_block)
    all_ids = lax.all_gather(ids, GROUP, axis=0, tiled=True)
    all_x = lax.all_gather(activations, GROUP, axis=0, tiled=True)
    mask = select_mask(all_ids - lax.axis_index(GROUP) * feat_block, feat_block)
    pre_acts = jnp.dot(all_x, enc_weight, preferred_element_type=jnp.float32) + enc_bias
    code_vals = jnp.where(mask > 0, pre_acts, 0.0).astype(jnp.bfloat16)
    partial_value = jnp.dot(code_vals, dec_weight, preferred_element_type=jnp.float32).astype(
        jnp.bfloat16
    )
    summed = lax.psum_scatter(partial_value, GROUP, scatter_dimension=0, tiled=True)
    residual = (summed.astype(jnp.float32) + dec_bias - activations.astype(jnp.float32)).astype(
        jnp.bfloat16
    )
    all_err = lax.all_gather(residual, GROUP, axis=0, tiled=True)
    grad_codes = lax.dot_general(
        all_err, dec_weight, (((1,), (1,)), ((), ())), preferred_element_type=jnp.float32
    )
    grad_pre = jnp.where(mask > 0, grad_codes, 0.0).astype(jnp.bfloat16)
    enc_grad = lax.dot_general(
        all_x, grad_pre, (((0,), (0,)), ((), ())), preferred_element_type=jnp.float32
    ).astype(jnp.bfloat16)
    raw_grad = lax.dot_general(
        code_vals, all_err, (((0,), (0,)), ((), ())), preferred_element_type=jnp.float32
    )
    dec_float = dec_weight.astype(jnp.float32)
    along_coef = jnp.sum(raw_grad * dec_float, axis=1) / (
        jnp.sum(dec_float * dec_float, axis=1) + 1e-06
    )
    dec_grad = (raw_grad - along_coef[:, None] * dec_float).astype(jnp.bfloat16)
    return (enc_grad, dec_grad)


def on_device(activations, block_lists, top_positions, *weights):
    owner_count = lax.axis_size(GROUP)
    pairs = activations.shape[0] * block_lists.shape[1]
    gathered = owner_count * activations.shape[0]
    if gathered <= 4 * pairs:
        return gathered_plan(activations, block_lists, top_positions, *weights)
    return routed_plan(activations, block_lists, top_positions, *weights)


def solution(mesh):
    placed = (
        P(("grp", "tok", "feat"), None),
        P(("grp", "tok", "feat"), None),
        P(("grp", "tok", "feat"), None),
        P(None, ("tok", "feat")),
        P(("tok", "feat")),
        P(("tok", "feat"), None),
        P(),
    )
    return jax.shard_map(
        on_device,
        mesh=mesh,
        in_specs=placed,
        out_specs=(P(None, ("grp", "tok", "feat")), P(("grp", "tok", "feat"), None)),
        check_vma=False,
    )
```

profile of v0, /device:TPU:0, one launch (start us, length us, event | category | flops | bytes accessed | tf_op | source)
XLA Modules:
  0.0 425.1 jit_solution(17819520309938272814)
XLA Ops:
  7.2 0.0 copy-start
  7.2 0.0 all-gather.3.cloned.1.call-start
  7.2 0.7 all-gather.3.cloned.1.call-update
  7.9 0.0 reduce-scatter.2.cloned.1.call-start
  8.0 0.9 copy.20
  8.9 0.2 slice_reduce_fusion.3
  9.2 0.8 fusion.11
  10.0 45.2 %all_gather.9 = s32[2048,64]{0,1:T(8,128)S(1)} all-gather(s32[128,64]{0,1:T(8,128)S(1)} %fusion.11), channel_id=1, replica_groups=mesh['grp'=2,'tok'=4,'feat'=4] {'tok','feat'}, dimensions={0}, use_global_device_ids=true | all-gather | bytes 557056 | tf_op jit(solution)/shard_map/all_gather | solution.py:146
  55.2 0.4 fusion.8
  55.6 8.9 %select_reduce_fusion = s32[2048,64]{0,1:T(8,128)S(1)} fusion(s32[2048,64]{0,1:T(8,128)S(1)} %get-tuple-element.17, s32[2048,64]{0,1:T(8,128)S(1)} %get-tuple-element.16), kind=kLoop, calls=%fused_computation | loop fusion | flops 25034752 | bytes 1572864 | tf_op jit(solution)/shard_map/reduce_sum | solution.py:130
  64.5 0.0 copy-start.6
  64.6 2.5 fusion.5
  67.0 54.2 %all-gather.3.cloned.1.call-done = bf16[2048,3072]{1,0:T(8,128)(2,1)} async-done(((bf16[128,3072]{1,0:T(8,128)(2,1)}), bf16[2048,3072]{1,0:T(8,128)(2,1)}) %all-gather.3.cloned.1.call-update) | async-done | bytes 12582928 | tf_op jit(solution)/shard_map/all_gather | solution.py:147
  121.2 0.0 copy-done
  121.2 0.0 copy-done.6
  121.2 0.0 copy-start.3
  121.2 10.1 %select_convert_fusion.1 = bf16[2048,512]{1,0:T(8,128)(2,1)S(1)} fusion(pred[2048,512]{1,0:T(32,128)(4,1)} %fusion.5, bf16[2048,3072]{1,0:T(8,128)(2,1)} %all-gather.3.cloned.1.call-done, bf16[3072,512]{1,0:T(8,128)(2,1)S(1)} %copy-done, f32[512]{0:T(512)S(1)} %copy-done.6), kind=kOutput, calls=%fused_computation.12 | convolution fusion | flops 6445596672 | bytes 18876416 | tf_op jit(solution)/shard_map/dot_general | solution.py:149
  131.3 0.0 copy-start.7
  131.3 1.3 copy-done.7
  132.6 0.0 copy-done.3
  132.6 9.7 %convolution_convert_fusion = bf16[2048,3072]{1,0:T(8,128)(2,1)} fusion(bf16[2048,512]{1,0:T(8,128)(2,1)S(1)} %select_convert_fusion.1, bf16[512,3072]{1,0:T(8,128)(2,1)S(1)} %copy-done.3), kind=kOutput, calls=%fused_computation.2 | convolution fusion | flops 6448742400 | bytes 17825792 | tf_op jit(solution)/shard_map/dot_general | solution.py:151
  142.4 0.0 copy-start.2
  142.4 0.0 copy-start.5
  142.4 0.0 reduce-scatter.2.cloned.1.call-update
  142.4 0.0 all-gather.5.cloned.1.call-start
  142.5 133.0 %reduce-scatter.2.cloned.1.call-done = bf16[128,3072]{1,0:T(8,128)(2,1)} async-done(((bf16[2048,3072]{1,0:T(8,128)(2,1)}), bf16[128,3072]{1,0:T(8,128)(2,1)}) %reduce-scatter.2.cloned.1.call-update) | async-done | bytes 786448 | tf_op jit(solution)/shard_map/reduce_scatter | solution.py:154
  275.5 0.0 copy-done.2
  275.5 0.0 copy-done.5
  275.5 2.3 subtract_convert_fusion
  277.8 0.0 all-gather.5.cloned.1.call-update
  277.8 100.1 %all-gather.5.cloned.1.call-done = bf16[2048,3072]{1,0:T(8,128)(2,1)} async-done(((bf16[128,3072]{1,0:T(8,128)(2,1)}), bf16[2048,3072]{1,0:T(8,128)(2,1)}) %all-gather.5.cloned.1.call-update) | async-done | bytes 12582928 | tf_op jit(solution)/shard_map/all_gather | solution.py:158
  377.9 23.1 %fusion.4 = bf16[3072,512]{0,1:T(8,128)(2,1)S(1)} fusion(bf16[2048,3072]{1,0:T(8,128)(2,1)} %all-gather.3.cloned.1.call-done, pred[2048,512]{1,0:T(32,128)(4,1)} %fusion.5, bf16[2048,3072]{1,0:T(8,128)(2,1)} %all-gather.5.cloned.1.call-done, bf16[512,3072]{1,0:T(8,128)(2,1)} %param.12), kind=kOutput, calls=%fused_computation.14 | convolution fusion | flops 12888571904 | bytes 32505856 | tf_op jit(solution)/shard_map/dot_general | solution.py:163
  401.0 2.8 copy.21
  403.8 0.0 copy-start.4
  403.8 11.7 %fusion.1 = (f32[512]{0:T(512)S(1)}, f32[512]{0:T(512)S(1)}, f32[512,3072]{1,0:T(8,128)S(1)}) fusion(bf16[512,3072]{1,0:T(8,128)(2,1)} %param.12, bf16[2048,512]{1,0:T(8,128)(2,1)} %copy-done.7, bf16[2048,3072]{1,0:T(8,128)(2,1)} %all-gather.5.cloned.1.call-done), kind=kOutput, calls=%fused_computation.7 | convolution fusion | flops 6450314240 | bytes 24121344 | tf_op jit(solution)/shard_map/dot_general | solution.py:166
  415.5 0.0 copy-start.1
  415.5 0.0 copy-done.4
  415.5 3.1 fusion.3
  418.6 0.0 copy-done.1
  (3 shorter events, 0.0 us)
Async XLA Ops:
  7.2 114.0 %copy-start = (bf16[3072,512]{1,0:T(8,128)(2,1)S(1)}, bf16[3072,512]{1,0:T(8,128)(2,1)}, u32[]{:S(2)}) copy-start(bf16[3072,512]{1,0:T(8,128)(2,1)} %param.10) | copy-start | bytes 9437188
  7.2 114.0 %all-gather.3.cloned.1.call-start = ((), (), s32[]{:S(2)}) async-start(), calls=%async_computation.1 | async-start | bytes 13369344 | tf_op jit(solution)/shard_map/all_gather | solution.py:147
  7.9 267.6 %reduce-scatter.2.cloned.1.call-start = ((), (), s32[]{:S(2)}) async-start(), calls=%async_computation.2 | async-start | bytes 13369344 | tf_op jit(solution)/shard_map/reduce_scatter | solution.py:154
  64.5 56.7 %copy-start.6 = (f32[512]{0:T(512)S(1)}, f32[512]{0:T(512)}, u32[]{:S(2)}) copy-start(f32[512]{0:T(512)} %param.11) | copy-start | bytes 6148
  121.2 11.4 %copy-start.3 = (bf16[512,3072]{1,0:T(8,128)(2,1)S(1)}, bf16[512,3072]{1,0:T(8,128)(2,1)}, u32[]{:S(2)}) copy-start(bf16[512,3072]{1,0:T(8,128)(2,1)} %param.12) | copy-start | bytes 9437188
  131.3 1.3 copy-start.7
  142.4 133.1 %copy-start.2 = (bf16[128,3072]{1,0:T(8,128)(2,1)S(1)}, bf16[128,3072]{1,0:T(8,128)(2,1)}, u32[]{:S(2)}) copy-start(bf16[128,3072]{1,0:T(8,128)(2,1)} %param.7) | copy-start | bytes 2359300
  142.4 133.1 %copy-start.5 = (f32[3072]{0:T(1024)S(1)}, f32[3072]{0:T(1024)}, u32[]{:S(2)}) copy-start(f32[3072]{0:T(1024)} %param.13) | copy-start | bytes 36868
  142.4 235.5 %all-gather.5.cloned.1.call-start = ((), (), s32[]{:S(2)}) async-start(), calls=%async_computation.3 | async-start | bytes 13369344 | tf_op jit(solution)/shard_map/all_gather | solution.py:158
  403.8 11.7 %copy-start.4 = (bf16[512,3072]{1,0:T(8,128)(2,1)S(1)}, bf16[512,3072]{1,0:T(8,128)(2,1)}, u32[]{:S(2)}) copy-start(bf16[512,3072]{1,0:T(8,128)(2,1)} %param.12) | copy-start | bytes 9437188
  415.5 3.1 copy-start.1
Sparse Core Ops, SparseCore 0:
  10.3 110.8 all-gather.2
  142.5 132.9 reduce-scatter.1
  277.9 99.8 all-gather.4
where the time goes:
time: 425 us
  waiting for transfers between devices  288 us (68%)
  matrix products  57.1 us (13%)
  blocking collectives  45.2 us (11%)
  other arithmetic  15.5 us (4%)
  between operations  13.8 us (3%)
  local copies, waits for them, and re-layouts  5.31 us (1%)
    reduce_scatter x1, waiting for transfers between devices, gathered_plan(): lax.psum_scatter(partial_value, GROUP, scatter_dimension=0, tiled=True)  133 us
    all_gather x1, waiting for transfers between devices, gathered_plan(): all_err = lax.all_gather(residual, GROUP, axis=0, tiled=True)  100 us
    all_gather x1, waiting for transfers between devices, gathered_plan(): all_x = lax.all_gather(activations, GROUP, axis=0, tiled=True)  54.2 us
    all_gather x1, blocking collectives, gathered_plan(): all_ids = lax.all_gather(ids, GROUP, axis=0, tiled=True)  45.2 us
    dot_general x1, matrix products, gathered_plan(): lax.dot_general(all_x, grad_pre, (((0,), (0,)), ((), ())), preferred_elem...  23.1 us
    dot_general x1, matrix products, gathered_plan(): lax.dot_general(code_vals, all_err, (((0,), (0,)), ((), ())), preferred_e...  11.7 us
    dot_general x1, matrix products, gathered_plan(): jnp.dot(all_x, enc_weight, preferred_element_type=jnp.float32) + enc_bias  10.1 us
    dot_general x1, matrix products, gathered_plan(): jnp.dot(code_vals, dec_weight, preferred_element_type=jnp.float32)  9.73 us
  transfers between devices with their start and end apart: 3, of which 3 were waited for; matrix products, arithmetic and copies ran while one was open for 3% of the time, Pallas kernels for 0%

commit v1 on v0

--- a/solution.py
+++ b/solution.py
@@ -155,7 +155,22 @@
     residual = (summed.astype(jnp.float32) + dec_bias - activations.astype(jnp.float32)).astype(
         jnp.bfloat16
     )
-    all_err = lax.all_gather(residual, GROUP, axis=0, tiled=True)
+
+    def apply_the_block(u_in):
+        ax_name = GROUP
+        view_out, u1, all_rows = (lax.psum(1, ax_name), lax.axis_index(ax_name), u_in.shape[0])
+        now, v_next = (u_in, 1)
+        while v_next < view_out:
+            in_order = []
+            i = 0
+            while i < view_out:
+                in_order.append((i, (i - v_next) % view_out))
+                i += 1
+            now = jnp.concatenate([now, lax.ppermute(now, ax_name, in_order)], 0)
+            v_next = 2 * v_next
+        return jnp.roll(now, u1 * all_rows, axis=0)
+
+    all_err = apply_the_block(residual)
     grad_codes = lax.dot_general(
         all_err, dec_weight, (((1,), (1,)), ((), ())), preferred_element_type=jnp.float32
     )

time: 425 us -> 625 us (1.47)
  waiting for transfers between devices: 288 us -> 438 us
  local copies, waits for them, and re-layouts: 5.31 us -> 28.9 us
  matrix products: 57.1 us -> 69.1 us
  other arithmetic: 15.5 us -> 22.7 us
  starting transfers between devices: 0.12 us -> 6.54 us
    ppermute x0 -> x4, waiting for transfers between devices: none -> 251 us  [apply_the_block(): now = jnp.concatenate([now, lax.ppermute(now, ax_name, in_order)], 0)]
    all_gather x1 -> x0, waiting for transfers between devices: 100 us -> none  [gathered_plan(): all_err = lax.all_gather(residual, GROUP, axis=0, tiled=True)]
    unnamed x18 -> x40, local copies, waits for them, and re-layouts: 5.06 us -> 22.6 us
    dot_general x1, matrix products: 23.1 us -> 34.8 us  [gathered_plan(): lax.dot_general(all_x, grad_pre, (((0,), (0,)), ((), ())), preferred_elem...]
    ppermute x0 -> x4, starting transfers between devices: none -> 6.46 us  [apply_the_block(): now = jnp.concatenate([now, lax.ppermute(now, ax_name, in_order)], 0)]
  transfers between devices with their start and end apart: 3 -> 6, of which waited for: 3 -> 6; matrix products, arithmetic and copies ran while one was open for 3% -> 3% of each run, Pallas kernels for 0% -> 0%
where the time goes in v1:
time: 625 us
  waiting for transfers between devices  438 us (70%)
  matrix products  69.1 us (11%)
  blocking collectives  45.2 us (7%)
  local copies, waits for them, and re-layouts  28.9 us (5%)
  other arithmetic  22.7 us (4%)
  between operations  14.1 us (2%)
  starting transfers between devices  6.54 us (1%)
    ppermute x4, waiting for transfers between devices, apply_the_block(): now = jnp.concatenate([now, lax.ppermute(now, ax_name, in_order)], 0)  251 us
    reduce_scatter x1, waiting for transfers between devices, gathered_plan(): lax.psum_scatter(partial_value, GROUP, scatter_dimension=0, tiled=True)  133 us
    all_gather x1, waiting for transfers between devices, gathered_plan(): all_x = lax.all_gather(activations, GROUP, axis=0, tiled=True)  54.2 us
    all_gather x1, blocking collectives, gathered_plan(): all_ids = lax.all_gather(ids, GROUP, axis=0, tiled=True)  45.2 us
    dot_general x1, matrix products, gathered_plan(): lax.dot_general(all_x, grad_pre, (((0,), (0,)), ((), ())), preferred_elem...  34.8 us
    unnamed x40, local copies, waits for them, and re-layouts  22.6 us
  transfers between devices with their start and end apart: 6, of which 6 were waited for; matrix products, arithmetic and copies ran while one was open for 3% of the time, Pallas kernels for 0%

profile of v1, /device:TPU:0, one launch (start us, length us, event | category | flops | bytes accessed | tf_op | source)
XLA Modules:
  0.0 625.0 jit_solution(77615142418770893)
XLA Ops:
  7.2 0.0 copy-start
  7.2 0.0 all-gather.2.cloned.1.call-start
  7.2 0.7 all-gather.2.cloned.1.call-update
  7.9 0.0 reduce-scatter.2.cloned.1.call-start
  8.0 0.9 copy.20
  8.9 0.2 slice_reduce_fusion.3
  9.2 0.8 fusion.19
  10.0 45.2 %all_gather.6 = s32[2048,64]{0,1:T(8,128)S(1)} all-gather(s32[128,64]{0,1:T(8,128)S(1)} %fusion.19), channel_id=1, replica_groups=mesh['grp'=2,'tok'=4,'feat'=4] {'tok','feat'}, dimensions={0}, use_global_device_ids=true | all-gather | bytes 557056 | tf_op jit(solution)/shard_map/all_gather | solution.py:146
  55.2 0.4 fusion.16
  55.6 0.0 copy-start.12
  55.6 8.9 %select_reduce_fusion = s32[2048,64]{0,1:T(8,128)S(1)} fusion(s32[2048,64]{0,1:T(8,128)S(1)} %get-tuple-element.19, s32[2048,64]{0,1:T(8,128)S(1)} %get-tuple-element.18), kind=kLoop, calls=%fused_computation | loop fusion | flops 25034752 | bytes 1572864 | tf_op jit(solution)/shard_map/reduce_sum | solution.py:130
  64.6 2.5 fusion.13
  67.0 54.2 %all-gather.2.cloned.1.call-done = bf16[2048,3072]{1,0:T(8,128)(2,1)} async-done(((bf16[128,3072]{1,0:T(8,128)(2,1)}), bf16[2048,3072]{1,0:T(8,128)(2,1)}) %all-gather.2.cloned.1.call-update) | async-done | bytes 12582928 | tf_op jit(solution)/shard_map/all_gather | solution.py:147
  121.2 0.0 copy-done
  121.2 0.0 copy-done.12
  121.2 10.1 %select_convert_fusion.1 = bf16[2048,512]{1,0:T(8,128)(2,1)S(1)} fusion(pred[2048,512]{1,0:T(32,128)(4,1)} %fusion.13, bf16[2048,3072]{1,0:T(8,128)(2,1)} %all-gather.2.cloned.1.call-done, bf16[3072,512]{1,0:T(8,128)(2,1)S(1)} %copy-done, f32[512]{0:T(512)S(1)} %copy-done.12), kind=kOutput, calls=%fused_computation.17 | convolution fusion | flops 6445596672 | bytes 18876416 | tf_op jit(solution)/shard_map/dot_general | solution.py:149
  131.3 0.0 copy-start.13
  131.3 1.3 copy-done.13
  132.7 0.0 copy-done.9
  132.7 9.7 %convolution_convert_fusion = bf16[2048,3072]{1,0:T(8,128)(2,1)} fusion(bf16[2048,512]{1,0:T(8,128)(2,1)S(1)} %select_convert_fusion.1, bf16[512,3072]{1,0:T(8,128)(2,1)S(1)} %copy-done.9), kind=kOutput, calls=%fused_computation.2 | convolution fusion | flops 6448742400 | bytes 17825792 | tf_op jit(solution)/shard_map/dot_general | solution.py:151
  142.3 0.0 reduce-scatter.2.cloned.1.call-update
  142.3 133.0 %reduce-scatter.2.cloned.1.call-done = bf16[128,3072]{1,0:T(8,128)(2,1)} async-done(((bf16[2048,3072]{1,0:T(8,128)(2,1)}), bf16[128,3072]{1,0:T(8,128)(2,1)}) %reduce-scatter.2.cloned.1.call-update) | async-done | bytes 786448 | tf_op jit(solution)/shard_map/reduce_scatter | solution.py:154
  275.3 0.0 copy-done.8
  275.3 2.3 constant_dynamic-update-slice_fusion.9
  277.6 2.1 collective-permute-start
  279.7 16.8 %collective-permute-done = bf16[128,3072]{1,0:T(8,128)(2,1)S(1)} collective-permute-done((bf16[128,3072]{1,0:T(8,128)(2,1)S(1)}, bf16[128,3072]{1,0:T(8,128)(2,1)S(1)}, u32[]{:S(2)}, u32[]{:S(2)}) %collective-permute-start) | collective-permute-done | bytes 786464 | tf_op jit(solution)/shard_map/ppermute | solution.py:169
  296.5 0.1 pad_maximum_fusion.2
  296.6 1.6 collective-permute-start.1
  298.2 68.3 %collective-permute-done.1 = bf16[256,3072]{1,0:T(8,128)(2,1)S(1)} collective-permute-done((bf16[256,3072]{1,0:T(8,128)(2,1)S(1)}, bf16[256,3072]{1,0:T(8,128)(2,1)S(1)}, u32[]{:S(2)}, u32[]{:S(2)}) %collective-permute-start.1) | collective-permute-done | bytes 1572896 | tf_op jit(solution)/shard_map/ppermute | solution.py:169
  366.5 0.2 pad_maximum_fusion.1
  366.7 1.6 collective-permute-start.2
  368.3 34.8 %collective-permute-done.2 = bf16[512,3072]{1,0:T(8,128)(2,1)S(1)} collective-permute-done((bf16[512,3072]{1,0:T(8,128)(2,1)S(1)}, bf16[512,3072]{1,0:T(8,128)(2,1)S(1)}, u32[]{:S(2)}, u32[]{:S(2)}) %collective-permute-start.2) | collective-permute-done | bytes 3145760 | tf_op jit(solution)/shard_map/ppermute | solution.py:169
  403.1 3.1 pad_maximum_fusion
  406.2 1.2 collective-permute-start.3
  407.4 2.1 constant_dynamic-update-slice_fusion.8
  409.4 2.7 constant_dynamic-update-slice_fusion.7
  412.1 1.9 constant_dynamic-update-slice_fusion.6
  414.0 130.6 %collective-permute-done.3 = bf16[1024,3072]{1,0:T(8,128)(2,1)} collective-permute-done((bf16[1024,3072]{1,0:T(8,128)(2,1)}, bf16[1024,3072]{1,0:T(8,128)(2,1)}, u32[]{:S(2)}, u32[]{:S(2)}) %collective-permute-start.3) | collective-permute-done | bytes 6291488 | tf_op jit(solution)/shard_map/ppermute | solution.py:169
  544.6 5.9 constant_dynamic-update-slice_fusion.5
  550.5 1.0 constant_dynamic-update-slice_fusion.4
  551.5 0.9 constant_dynamic-update-slice_fusion.3
  552.4 1.3 constant_dynamic-update-slice_fusion.2
  553.7 1.9 constant_dynamic-update-slice_fusion.1
  555.5 6.0 constant_dynamic-update-slice_fusion
  561.5 12.1 %fusion.5 = (f32[512]{0:T(512)S(1)}, f32[512]{0:T(512)S(1)}, f32[512,3072]{1,0:T(8,128)}) fusion(bf16[512,3072]{1,0:T(8,128)(2,1)S(1)} %copy-done.10, bf16[2048,512]{1,0:T(8,128)(2,1)S(1)} %copy-done.14, bf16[4096,3072]{1,0:T(8,128)(2,1)} %constant_dynamic-update-slice_fusion, s32[]{:T(128)S(6)} %select_n.78), kind=kOutput, calls=%fused_computation.11 | convolution fusion | flops 6450314240 | bytes 24121348 | tf_op jit(solution)/shard_map/dot_general | solution.py:181
  573.6 34.8 %fusion.8 = bf16[3072,512]{0,1:T(8,128)(2,1)S(1)} fusion(bf16[2048,3072]{1,0:T(8,128)(2,1)} %all-gather.2.cloned.1.call-done, pred[2048,512]{1,0:T(32,128)(4,1)} %fusion.13, bf16[512,3072]{1,0:T(8,128)(2,1)} %param.12, bf16[4096,3072]{1,0:T(8,128)(2,1)} %constant_dynamic-update-slice_fusion, s32[]{:T(128)S(6)} %select_n.78), kind=kOutput, calls=%fused_computation.19 | convolution fusion | flops 12888571904 | bytes 32505860 | tf_op jit(solution)/shard_map/dot_general | solution.py:178
  608.4 2.8 copy.21
  611.2 6.9 %fusion.7 = bf16[512,3072]{1,0:T(8,128)(2,1)} fusion(f32[512,3072]{1,0:T(8,128)} %get-tuple-element.20, bf16[512,3072]{1,0:T(8,128)(2,1)} %param.12, f32[512]{0:T(512)S(1)} %add_divide_fusion), kind=kLoop, calls=%fused_computation.13 | loop fusion | flops 6291456 | bytes 12584960 | tf_op jit(solution)/shard_map/convert_element_type | solution.py:188
  (25 shorter events, 0.1 us)
Async XLA Ops:
  7.2 114.0 %copy-start = (bf16[3072,512]{1,0:T(8,128)(2,1)S(1)}, bf16[3072,512]{1,0:T(8,128)(2,1)}, u32[]{:S(2)}) copy-start(bf16[3072,512]{1,0:T(8,128)(2,1)} %param.10) | copy-start | bytes 9437188
  7.2 114.0 %all-gather.2.cloned.1.call-start = ((), (), s32[]{:S(2)}) async-start(), calls=%async_computation.1 | async-start | bytes 13369344 | tf_op jit(solution)/shard_map/all_gather | solution.py:147
  7.9 267.4 %reduce-scatter.2.cloned.1.call-start = ((), (), s32[]{:S(2)}) async-start(), calls=%async_computation.2 | async-start | bytes 13369344 | tf_op jit(solution)/shard_map/reduce_scatter | solution.py:154
  55.6 65.6 %copy-start.12 = (f32[512]{0:T(512)S(1)}, f32[512]{0:T(512)}, u32[]{:S(2)}) copy-start(f32[512]{0:T(512)} %param.11) | copy-start | bytes 6148
  121.2 11.5 %copy-start.9 = (bf16[512,3072]{1,0:T(8,128)(2,1)S(1)}, bf16[512,3072]{1,0:T(8,128)(2,1)}, u32[]{:S(2)}) copy-start(bf16[512,3072]{1,0:T(8,128)(2,1)} %param.12) | copy-start | bytes 9437188
  131.3 1.3 copy-start.13
  142.3 133.0 %copy-start.8 = (bf16[128,3072]{1,0:T(8,128)(2,1)S(1)}, bf16[128,3072]{1,0:T(8,128)(2,1)}, u32[]{:S(2)}) copy-start(bf16[128,3072]{1,0:T(8,128)(2,1)} %param.7) | copy-start | bytes 2359300
  142.3 133.0 %copy-start.11 = (f32[3072]{0:T(1024)S(1)}, f32[3072]{0:T(1024)}, u32[]{:S(2)}) copy-start(f32[3072]{0:T(1024)} %param.13) | copy-start | bytes 36868
  277.6 128.6 %copy-start.4 = (bf16[128,3072]{1,0:T(8,128)(2,1)}, bf16[128,3072]{1,0:T(8,128)(2,1)S(1)}, u32[]{:S(2)}) copy-start(bf16[128,3072]{1,0:T(8,128)(2,1)S(1)} %get-tuple-element.17) | copy-start | bytes 2359300
  277.6 18.9 %collective-permute-start = (bf16[128,3072]{1,0:T(8,128)(2,1)S(1)}, bf16[128,3072]{1,0:T(8,128)(2,1)S(1)}, u32[]{:S(2)}, u32[]{:S(2)}) collective-permute-start(bf16[128,3072]{1,0:T(8,128)(2,1)S(1)} %get-tuple-element.17), channel_id=1, source_target_pairs={{0,15},{1,0},{2,1},{3,2},{4,3},{5,4},{6,5},{7,6},{8,7},{9,8},{10,9... | collective-permute-start | bytes 2359304 | tf_op jit(solution)/shard_map/ppermute | solution.py:169
  296.5 109.7 %copy-start.6 = (bf16[128,3072]{1,0:T(8,128)(2,1)}, bf16[128,3072]{1,0:T(8,128)(2,1)S(1)}, u32[]{:S(2)}) copy-start(bf16[128,3072]{1,0:T(8,128)(2,1)S(1)} %collective-permute-done) | copy-start | bytes 2359300
  296.6 69.9 %collective-permute-start.1 = (bf16[256,3072]{1,0:T(8,128)(2,1)S(1)}, bf16[256,3072]{1,0:T(8,128)(2,1)S(1)}, u32[]{:S(2)}, u32[]{:S(2)}) collective-permute-start(bf16[256,3072]{1,0:T(8,128)(2,1)S(1)} %pad_maximum_fusion.2), channel_id=1, source_target_pairs={{0,14},{1,15},{2,0},{3,1},{4,2},{5,3},{6,4},{7,5},{8,6},{9,7},{10,... | collective-permute-start | bytes 4718600 | tf_op jit(solution)/shard_map/ppermute | solution.py:169
  366.5 39.7 %copy-start.2 = (bf16[256,3072]{1,0:T(8,128)(2,1)}, bf16[256,3072]{1,0:T(8,128)(2,1)S(1)}, u32[]{:S(2)}) copy-start(bf16[256,3072]{1,0:T(8,128)(2,1)S(1)} %collective-permute-done.1) | copy-start | bytes 4718596
  366.7 36.4 %collective-permute-start.2 = (bf16[512,3072]{1,0:T(8,128)(2,1)S(1)}, bf16[512,3072]{1,0:T(8,128)(2,1)S(1)}, u32[]{:S(2)}, u32[]{:S(2)}) collective-permute-start(bf16[512,3072]{1,0:T(8,128)(2,1)S(1)} %pad_maximum_fusion.1), channel_id=1, source_target_pairs={{0,12},{1,13},{2,14},{3,15},{4,0},{5,1},{6,2},{7,3},{8,4},{9,5},{1... | collective-permute-start | bytes 9437192 | tf_op jit(solution)/shard_map/ppermute | solution.py:169
  406.2 138.4 %collective-permute-start.3 = (bf16[1024,3072]{1,0:T(8,128)(2,1)}, bf16[1024,3072]{1,0:T(8,128)(2,1)}, u32[]{:S(2)}, u32[]{:S(2)}) collective-permute-start(bf16[1024,3072]{1,0:T(8,128)(2,1)} %pad_maximum_fusion), channel_id=1, source_target_pairs={{0,8},{1,9},{2,10},{3,11},{4,12},{5,13},{6,14},{7,15},{8,0},{9,1},... | collective-permute-start | bytes 18874376 | tf_op jit(solution)/shard_map/ppermute | solution.py:169
  414.0 136.5 %copy-start.5 = (bf16[128,3072]{1,0:T(8,128)(2,1)S(1)}, bf16[128,3072]{1,0:T(8,128)(2,1)}, u32[]{:S(2)}) copy-start(bf16[128,3072]{1,0:T(8,128)(2,1)} %copy-done.4) | copy-start | bytes 2359300
  414.0 137.5 %copy-start.7 = (bf16[128,3072]{1,0:T(8,128)(2,1)S(1)}, bf16[128,3072]{1,0:T(8,128)(2,1)}, u32[]{:S(2)}) copy-start(bf16[128,3072]{1,0:T(8,128)(2,1)} %copy-done.6) | copy-start | bytes 2359300
  414.0 138.4 %copy-start.3 = (bf16[256,3072]{1,0:T(8,128)(2,1)S(1)}, bf16[256,3072]{1,0:T(8,128)(2,1)}, u32[]{:S(2)}) copy-start(bf16[256,3072]{1,0:T(8,128)(2,1)} %copy-done.2) | copy-start | bytes 4718596
  555.5 6.0 copy-start.10
  555.5 6.0 copy-start.14
  611.2 6.9 %copy-start.1 = (bf16[3072,512]{1,0:T(8,128)(2,1)S(1)}, bf16[3072,512]{1,0:T(8,128)(2,1)}, u32[]{:S(2)}) copy-start(bf16[3072,512]{1,0:T(8,128)(2,1)} %param.10) | copy-start | bytes 9437188
Sparse Core Ops, SparseCore 0:
  10.3 110.8 all-gather.1
  142.5 132.7 reduce-scatter.1
